TPU v7x, 512 devices: a whole 4x8x8 slice. The times are simulated.
512 devices in a mesh: row: 32 (over y, z_lo), col: 16 (over z_hi, x, core).
Axes of the slice: x: 4, y: 8, z: 8 (z_hi: 2, z_lo: 4; z = z_hi * 4 + z_lo), core: 2. Of those that a mesh axis runs over, the one named last changes fastest.
Arguments:
- table: float32 [16, 256, 256], P('col', 'row'), may hold values from -4 to 4
- marginals: int32 [4096], replicated, may hold values from 64 to 4095
- visits: int32 [32, 16, 16], P('row', 'col'), may hold values from 0 to 15
- counts: int32 [32, 16, 16, 256, 256], P('row', 'col'), may hold values from 0 to 16, as said below
Outputs:
- gradient: float32 [16, 256, 256], P('col')
Inputs may be any that keep to these rules, and one draw needn't show every extreme that they name: `counts`: about half of the cells of every tile are zero.
All inputs are finite; a program needn't handle non-finite values.
Results may differ from a plain program's by a relative error of at most 0.0031.
Values may be sent and summed in bfloat16 or wider, within the bound.
A program may use at most 128 MiB of HBM per device.

v0:
```python
import jax
import jax.numpy as jnp
from jax import lax
from jax.sharding import PartitionSpec as P

K = 16
LOSS_SCALE = 0.0625


def from_root(value, axis, source):
    kept = jnp.where(lax.axis_index(axis) == source, value, 0).astype(value.dtype)
    return lax.psum(kept, axis)


def tile_terms(row_vectors, col_vectors, count_tile, log_rows, log_cols, log_total):
    logits = lax.dot_general(
        row_vectors, col_vectors, (((1,), (1,)), ((), ())), preferred_element_type=jnp.float32
    )
    count_vals = count_tile.astype(jnp.float32)
    baseline = log_total - log_rows[:, None] - log_cols[None, :]
    margin = logits - baseline
    fitted = (0.1 + 0.25 * jnp.sqrt(count_vals)) * (margin - jnp.log(jnp.maximum(count_vals, 1.0)))
    soft_hinge = jax.nn.sigmoid(margin)
    grad_logits = (jnp.where(count_vals > 0, fitted, soft_hinge) * LOSS_SCALE).astype(jnp.bfloat16)
    row_term = jnp.dot(grad_logits, col_vectors, preferred_element_type=jnp.float32)
    col_term = lax.dot_general(
        grad_logits, row_vectors, (((0,), (0,)), ((), ())), preferred_element_type=jnp.float32
    )
    return (row_term, col_term)


def local(table, marginals, visits, counts):
    blocks = lax.axis_size("col")
    row_devices = lax.axis_size("row")
    own_block = lax.axis_index("row") % blocks
    pieces = table.astype(jnp.bfloat16)
    block_rows = pieces.shape[1] * row_devices
    embed_width = pieces.shape[2]
    log_marg = jnp.log(marginals.astype(jnp.float32)).reshape(blocks, block_rows)
    log_total = jnp.log(jnp.sum(marginals).astype(jnp.float32))
    visited = visits[0, 0]
    count_tiles = counts[0, 0]
    log_rows = log_marg[own_block]
    zero_block = jnp.zeros((block_rows, embed_width), jnp.float32)
    col_block = lax.all_gather(pieces, "row", axis=1, tiled=True)
    row_vectors = from_root(col_block, "col", own_block)[0]
    start_terms = jnp.zeros((K, block_rows, embed_width), jnp.float32)
    shards = lax.all_gather(col_block, "col", axis=0, tiled=True)
    visit_row_sum = zero_block
    visit_col_terms = start_terms
    for k in range(K):
        visit_id = visited[k]
        inside = (visit_id >= 0) & (visit_id < shards.shape[0])
        col_vectors = lax.dynamic_index_in_dim(
            shards, jnp.clip(visit_id, 0, shards.shape[0] - 1), 0, keepdims=False
        )

        def compute(vectors, tile_k=count_tiles[k], log_cols=log_marg[visit_id]):
            return tile_terms(row_vectors, vectors, tile_k, log_rows, log_cols, log_total)

        def skipped(vectors):
            return (zero_block, zero_block)

        row_term, col_term = lax.cond(inside, compute, skipped, col_vectors)
        visit_row_sum = visit_row_sum + row_term
        visit_col_terms = visit_col_terms.at[k].add(col_term)
    block_ids = jnp.arange(1 * lax.axis_size("col"), dtype=jnp.int32)
    result = jnp.zeros((1 * lax.axis_size("col"), block_rows, embed_width), jnp.float32)
    for dense_k in range(K):
        result = result + jnp.where(
            (block_ids == visited[dense_k])[:, None, None], visit_col_terms[dense_k][None], 0.0
        )
    result = result + jnp.where((block_ids == own_block)[:, None, None], visit_row_sum[None], 0.0)
    summed = lax.psum_scatter(result, "col", scatter_dimension=0, tiled=True)
    return lax.psum(summed, "row")


def solution(mesh):
    return jax.shard_map(
        local,
        mesh=mesh,
        in_specs=(
            P("col", "row", None),
            P(),
            P("row", "col", None),
            P("row", "col", None, None, None),
        ),
        out_specs=P("col", None, None),
        check_vma=False,
    )
```

profile of v0, /device:TPU:2, one launch (start us, length us, event | category | flops | bytes accessed | tf_op | source)
XLA Modules:
  0.0 988.8 jit_solution(14721961554316318443)
XLA Ops:
  7.2 82.3 %all_gather.6 = bf16[1,256,256]{2,1,0:T(8,128)(2,1)S(1)} all-gather(bf16[1,8,256]{2,1,0:T(8,128)(2,1)S(1)} %convert_element_type.204), channel_id=1, replica_groups=mesh['row'=32,'col'=16] {'row'}, dimensions={1}, use_global_device_ids=true | all-gather | bytes 135168 | tf_op jit(solution)/shard_map/all_gather | solution.py:45
  91.1 2.0 fusion.207
  112.9 1.4 reduce_sum.9
  117.5 1.8 iota_compare_fusion.3
  119.4 1.8 iota_compare_fusion.5
  121.2 1.8 iota_compare_fusion.7
  123.0 1.7 iota_compare_fusion.9
  124.6 1.8 iota_compare_fusion.11
  126.4 1.8 iota_compare_fusion.13
  128.2 1.9 iota_compare_fusion.15
  130.1 135.8 %all-reduce.4.cloned.1.call-done = bf16[256,256]{1,0:T(8,128)(2,1)} async-done(((bf16[256,256]{1,0:T(8,128)(2,1)}), bf16[256,256]{1,0:T(8,128)(2,1)}) %all-reduce.4.cloned.1.call-update) | async-done | bytes 131088 | tf_op jit(solution)/shard_map/psum | solution.py:12
  265.9 79.2 %all-gather.2.cloned.1.call-done = bf16[16,256,256]{2,1,0:T(8,128)(2,1)} async-done(((bf16[1,256,256]{2,1,0:T(8,128)(2,1)}), bf16[16,256,256]{2,1,0:T(8,128)(2,1)}) %all-gather.2.cloned.1.call-update) | async-done | bytes 2097168 | tf_op jit(solution)/shard_map/all_gather | solution.py:48
  345.1 13.3 %conditional.16 = (f32[256,256]{1,0:T(8,128)S(1)}, f32[16,256,256]{2,1,0:T(8,128)}) conditional(s32[]{:T(128)} %convert_element_type.203, () %tuple.261, (s32[1,1,16,256,256]{4,3,2,1,0:T(8,128)}, s32[]{:T(128)}, bf16[16,256,256]{2,1,0:T(8,128)(2,1)}, bf16[256,256]{1,0:T(8,128)(2,1)}, f32[]{:T(128)}, /*index=5*/f32[1,256]{1,0:T(1,128)S(1)}, ...), branch_computations={%region_2.3_spmd, %region_3.4_spmd} | conditional | flops 101646592 | bytes 15079546 | solution.py:64
  347.8 5.4 copy.21
  353.2 1.4 fusion.4
  354.8 2.4 scatter-add.14
  358.4 10.6 %conditional.17 = (f32[256,256]{1,0:T(8,128)S(1)}, f32[1,256,256]{2,1,0:T(8,128)S(1)}) conditional(s32[]{:T(128)} %convert_element_type.207, () %tuple.263, (s32[1,1,16,256,256]{4,3,2,1,0:T(8,128)}, s32[]{:T(128)}, bf16[16,256,256]{2,1,0:T(8,128)(2,1)}, bf16[256,256]{1,0:T(8,128)(2,1)}, f32[]{:T(128)}, /*index=5*/f32[1,256]{1,0:T(1,128)S(1)}, ...), branch_computations={%region_4.5_spmd, %region_5.6_spmd} | conditional | flops 101646592 | bytes 10623094 | solution.py:64
  360.9 5.4 copy.22
  369.8 10.9 %conditional.18 = (f32[256,256]{1,0:T(8,128)S(1)}, f32[1,256,256]{2,1,0:T(8,128)S(1)}) conditional(s32[]{:T(128)} %convert_element_type.208, () %tuple.265, (s32[1,1,16,256,256]{4,3,2,1,0:T(8,128)}, s32[]{:T(128)}, bf16[16,256,256]{2,1,0:T(8,128)(2,1)}, bf16[256,256]{1,0:T(8,128)(2,1)}, f32[]{:T(128)}, /*index=5*/f32[1,256]{1,0:T(1,128)S(1)}, ...), branch_computations={%region_6.7_spmd, %region_7.8_spmd} | conditional | flops 101646592 | bytes 10623094 | solution.py:64
  372.5 5.4 copy.23
  380.7 1.7 fusion.204
  382.4 10.6 %conditional.19 = (f32[256,256]{1,0:T(8,128)S(1)}, f32[1,256,256]{2,1,0:T(8,128)S(1)}) conditional(s32[]{:T(128)} %convert_element_type.209, () %tuple.267, (s32[1,1,16,256,256]{4,3,2,1,0:T(8,128)}, s32[]{:T(128)}, bf16[16,256,256]{2,1,0:T(8,128)(2,1)}, bf16[256,256]{1,0:T(8,128)(2,1)}, f32[]{:T(128)}, /*index=5*/f32[1,256]{1,0:T(1,128)S(1)}, ...), branch_computations={%region_8.9_spmd, %region_9.10_spmd} | conditional | flops 101646592 | bytes 10623094 | solution.py:64
  384.9 5.4 copy.24
  393.0 1.7 fusion.203
  394.7 10.6 %conditional.20 = (f32[256,256]{1,0:T(8,128)S(1)}, f32[1,256,256]{2,1,0:T(8,128)S(1)}) conditional(s32[]{:T(128)} %convert_element_type.210, () %tuple.269, (s32[1,1,16,256,256]{4,3,2,1,0:T(8,128)}, s32[]{:T(128)}, bf16[16,256,256]{2,1,0:T(8,128)(2,1)}, bf16[256,256]{1,0:T(8,128)(2,1)}, f32[]{:T(128)}, /*index=5*/f32[1,256]{1,0:T(1,128)S(1)}, ...), branch_computations={%region_10.11_spmd, %region_11.12_spmd} | conditional | flops 101646592 | bytes 10623094 | solution.py:64
  397.2 5.4 copy.25
  405.3 1.7 fusion.202
  407.0 10.4 %conditional.21 = (f32[256,256]{1,0:T(8,128)S(1)}, f32[1,256,256]{2,1,0:T(8,128)S(1)}) conditional(s32[]{:T(128)} %convert_element_type.211, () %tuple.271, (s32[1,1,16,256,256]{4,3,2,1,0:T(8,128)}, s32[]{:T(128)}, bf16[16,256,256]{2,1,0:T(8,128)(2,1)}, bf16[256,256]{1,0:T(8,128)(2,1)}, f32[]{:T(128)}, /*index=5*/f32[1,256]{1,0:T(1,128)S(1)}, ...), branch_computations={%region_12.13_spmd, %region_13.14_spmd} | conditional | flops 101646592 | bytes 10623094 | solution.py:64
  409.3 5.4 copy.26
  417.4 1.7 fusion.201
  419.1 10.4 %conditional.22 = (f32[256,256]{1,0:T(8,128)S(1)}, f32[1,256,256]{2,1,0:T(8,128)S(1)}) conditional(s32[]{:T(128)} %convert_element_type.212, () %tuple.273, (s32[1,1,16,256,256]{4,3,2,1,0:T(8,128)}, s32[]{:T(128)}, bf16[16,256,256]{2,1,0:T(8,128)(2,1)}, bf16[256,256]{1,0:T(8,128)(2,1)}, f32[]{:T(128)}, /*index=5*/f32[1,256]{1,0:T(1,128)S(1)}, ...), branch_computations={%region_14.15_spmd, %region_15.16_spmd} | conditional | flops 101646592 | bytes 10623094 | solution.py:64
  421.4 5.4 copy.27
  429.5 1.7 fusion.200
  431.2 10.4 %conditional.23 = (f32[256,256]{1,0:T(8,128)S(1)}, f32[1,256,256]{2,1,0:T(8,128)S(1)}) conditional(s32[]{:T(128)} %convert_element_type.213, () %tuple.275, (s32[1,1,16,256,256]{4,3,2,1,0:T(8,128)}, s32[]{:T(128)}, bf16[16,256,256]{2,1,0:T(8,128)(2,1)}, bf16[256,256]{1,0:T(8,128)(2,1)}, f32[]{:T(128)}, /*index=5*/f32[1,256]{1,0:T(1,128)S(1)}, ...), branch_computations={%region_16.17_spmd, %region_17.18_spmd} | conditional | flops 101646592 | bytes 10623094 | solution.py:64
  433.5 5.4 copy.28
  441.6 1.7 fusion.199
  443.3 10.8 %conditional.24 = (f32[256,256]{1,0:T(8,128)S(1)}, f32[1,256,256]{2,1,0:T(8,128)S(1)}) conditional(s32[]{:T(128)} %convert_element_type.214, () %tuple.277, (s32[1,1,16,256,256]{4,3,2,1,0:T(8,128)}, s32[]{:T(128)}, bf16[16,256,256]{2,1,0:T(8,128)(2,1)}, bf16[256,256]{1,0:T(8,128)(2,1)}, f32[]{:T(128)}, /*index=5*/f32[1,256]{1,0:T(1,128)S(1)}, ...), branch_computations={%region_18.19_spmd, %region_19.20_spmd} | conditional | flops 101646592 | bytes 10623094 | solution.py:64
  446.0 5.4 copy.29
  454.1 1.7 fusion.198
  455.8 10.6 %conditional.25 = (f32[256,256]{1,0:T(8,128)S(1)}, f32[1,256,256]{2,1,0:T(8,128)S(1)}) conditional(s32[]{:T(128)} %convert_element_type.215, () %tuple.279, (s32[1,1,16,256,256]{4,3,2,1,0:T(8,128)}, s32[]{:T(128)}, bf16[16,256,256]{2,1,0:T(8,128)(2,1)}, bf16[256,256]{1,0:T(8,128)(2,1)}, f32[]{:T(128)}, /*index=5*/f32[1,256]{1,0:T(1,128)S(1)}, ...), branch_computations={%region_20.21_spmd, %region_21.22_spmd} | conditional | flops 101646592 | bytes 10623094 | solution.py:64
  458.3 5.4 copy.30
  466.4 1.7 fusion.197
  468.2 10.5 %conditional.26 = (f32[256,256]{1,0:T(8,128)S(1)}, f32[1,256,256]{2,1,0:T(8,128)S(1)}) conditional(s32[]{:T(128)} %convert_element_type.216, () %tuple.281, (s32[1,1,16,256,256]{4,3,2,1,0:T(8,128)}, s32[]{:T(128)}, bf16[16,256,256]{2,1,0:T(8,128)(2,1)}, bf16[256,256]{1,0:T(8,128)(2,1)}, f32[]{:T(128)}, /*index=5*/f32[1,256]{1,0:T(1,128)S(1)}, ...), branch_computations={%region_22.23_spmd, %region_23.24_spmd} | conditional | flops 101646592 | bytes 10623094 | solution.py:64
  470.5 5.4 copy.31
  478.6 1.7 fusion.196
  480.3 10.9 %conditional.27 = (f32[256,256]{1,0:T(8,128)S(1)}, f32[1,256,256]{2,1,0:T(8,128)S(1)}) conditional(s32[]{:T(128)} %convert_element_type.217, () %tuple.283, (s32[1,1,16,256,256]{4,3,2,1,0:T(8,128)}, s32[]{:T(128)}, bf16[16,256,256]{2,1,0:T(8,128)(2,1)}, bf16[256,256]{1,0:T(8,128)(2,1)}, f32[]{:T(128)}, /*index=5*/f32[1,256]{1,0:T(1,128)S(1)}, ...), branch_computations={%region_24.25_spmd, %region_25.26_spmd} | conditional | flops 101646592 | bytes 10623094 | solution.py:64
  483.1 5.4 copy.32
  491.3 1.7 fusion.195
  493.0 12.3 %conditional.28 = (f32[256,256]{1,0:T(8,128)S(1)}, f32[1,256,256]{2,1,0:T(8,128)}) conditional(s32[]{:T(128)} %convert_element_type.218, () %tuple.285, (s32[1,1,16,256,256]{4,3,2,1,0:T(8,128)}, s32[]{:T(128)}, bf16[16,256,256]{2,1,0:T(8,128)(2,1)}, bf16[256,256]{1,0:T(8,128)(2,1)}, f32[]{:T(128)}, /*index=5*/f32[1,256]{1,0:T(1,128)S(1)}, ...), branch_computations={%region_26.27_spmd, %region_27.28_spmd} | conditional | flops 101646592 | bytes 10623094 | solution.py:64
  496.4 5.4 copy.33
  505.3 1.9 fusion.205
  507.1 13.3 %conditional.29 = (f32[256,256]{1,0:T(8,128)}, f32[1,256,256]{2,1,0:T(8,128)}) conditional(s32[]{:T(128)} %convert_element_type.219, () %tuple.287, (s32[1,1,16,256,256]{4,3,2,1,0:T(8,128)}, s32[]{:T(128)}, bf16[16,256,256]{2,1,0:T(8,128)(2,1)}, bf16[256,256]{1,0:T(8,128)(2,1)}, f32[]{:T(128)}, /*index=5*/f32[1,256]{1,0:T(1,128)S(1)}, ...), branch_computations={%region_28.29_spmd, %region_29.30_spmd} | conditional | flops 101646592 | bytes 10623094 | solution.py:64
  511.0 5.4 copy.34
  518.6 1.8 fusion.161
  520.5 13.3 %conditional.30 = (f32[256,256]{1,0:T(8,128)}, f32[1,256,256]{2,1,0:T(8,128)}) conditional(s32[]{:T(128)} %convert_element_type.220, () %tuple.289, (s32[1,1,16,256,256]{4,3,2,1,0:T(8,128)}, s32[]{:T(128)}, bf16[16,256,256]{2,1,0:T(8,128)(2,1)}, bf16[256,256]{1,0:T(8,128)(2,1)}, f32[]{:T(128)}, /*index=5*/f32[1,256]{1,0:T(1,128)S(1)}, ...), branch_computations={%region_30.31_spmd, %region_31.32_spmd} | conditional | flops 101646592 | bytes 10623094 | solution.py:64
  524.3 5.4 copy.35
  531.9 1.9 fusion.173
  533.8 11.7 %conditional.31 = (f32[256,256]{1,0:T(8,128)S(1)}, f32[1,256,256]{2,1,0:T(8,128)S(1)}) conditional(s32[]{:T(128)} %convert_element_type.221, () %tuple.291, (s32[1,1,16,256,256]{4,3,2,1,0:T(8,128)}, s32[]{:T(128)}, bf16[16,256,256]{2,1,0:T(8,128)(2,1)}, bf16[256,256]{1,0:T(8,128)(2,1)}, f32[]{:T(128)}, /*index=5*/f32[1,256]{1,0:T(1,128)S(1)}, ...), branch_computations={%region_32.33_spmd, %region_33.34_spmd} | conditional | flops 101646592 | bytes 10627218 | solution.py:64
  537.4 5.4 copy.36
  546.3 2.8 slice_bitcast_fusion.11
  550.7 11.3 %select_add_fusion = f32[16,256,256]{2,1,0:T(8,128)} fusion(f32[256,256]{1,0:T(8,128)S(1)} %add_add_fusion, f32[256,256]{1,0:T(8,128)S(1)} %get-tuple-element.1640, f32[256,256]{1,0:T(8,128)S(1)} %get-tuple-element.1641, f32[256,256]{1,0:T(8,128)S(1)} %get-tuple-element.1642, f32[256,256]{1,0:T(8,128)S(1)} %copy-done.20, ...), kind=kLoop, calls=%fused_computation.288 | loop fusion | flops 34603008 | bytes 8651024 | tf_op jit(solution)/shard_map/add | solution.py:73
  562.1 109.4 %reduce-scatter.2.cloned.1.call-done = f32[1,256,256]{2,1,0:T(8,128)} async-done(((f32[16,256,256]{2,1,0:T(8,128)}), f32[1,256,256]{2,1,0:T(8,128)}) %reduce-scatter.2.cloned.1.call-update) | async-done | bytes 262160 | tf_op jit(solution)/shard_map/reduce_scatter | solution.py:74
  671.6 309.0 %all-reduce.6.cloned.1.call-done = f32[1,256,256]{2,1,0:T(8,128)} async-done(((f32[1,256,256]{2,1,0:T(8,128)}), f32[1,256,256]{2,1,0:T(8,128)}) %all-reduce.6.cloned.1.call-update) | async-done | bytes 262160 | tf_op jit(solution)/shard_map/psum | solution.py:75
  980.6 1.7 copy.115
  (152 shorter events, 53.6 us)
Async XLA Ops:
  6.5 259.4 %all-reduce.4.cloned.1.call-start = ((), (), s32[]{:S(2)}) async-start(), calls=%async_computation.2 | async-start | bytes 262144 | tf_op jit(solution)/shard_map/psum | solution.py:12
  89.5 0.8 copy-start.16
  90.3 254.8 %all-gather.2.cloned.1.call-start = ((), (), s32[]{:S(2)}) async-start(), calls=%async_computation.1 | async-start | bytes 2228224 | tf_op jit(solution)/shard_map/all_gather | solution.py:48
  91.0 580.5 %reduce-scatter.2.cloned.1.call-start = ((), (), s32[]{:S(2)}) async-start(), calls=%async_computation.3 | async-start | bytes 4456448 | tf_op jit(solution)/shard_map/reduce_scatter | solution.py:74
  115.1 365.3 %copy-start.21 = (f32[16,256]{1,0:T(8,128)}, f32[16,256]{1,0:T(8,128)S(1)}, u32[]{:S(2)}) copy-start(f32[16,256]{1,0:T(8,128)S(1)} %reshape.989) | copy-start | bytes 49156
  347.8 5.4 copy-start
  360.9 5.4 copy-start.1
  372.5 5.4 copy-start.2
  384.9 5.4 copy-start.3
  397.2 5.4 copy-start.4
  409.3 5.4 copy-start.5
  421.4 5.4 copy-start.6
  433.5 5.4 copy-start.7
  446.0 5.4 copy-start.8
  458.3 5.4 copy-start.9
  470.5 5.4 copy-start.10
  483.1 5.4 copy-start.11
  496.4 5.4 copy-start.12
  511.0 5.4 copy-start.13
  524.2 5.4 copy-start.14
  537.3 5.5 copy-start.15
  537.3 5.5 copy-start.35
  545.5 0.7 copy-start.17
  545.5 0.8 copy-start.19
  546.3 3.0 copy-start.18
  549.1 1.5 copy-start.20
  549.1 1.5 copy-start.22
  549.1 1.5 copy-start.23
  549.1 1.5 copy-start.24
  549.2 1.5 copy-start.25
  549.2 1.5 copy-start.26
  549.2 1.5 copy-start.27
  549.2 1.5 copy-start.28
  549.2 1.5 copy-start.29
  549.2 1.5 copy-start.30
  549.2 1.5 copy-start.31
  549.2 1.5 copy-start.32
  549.2 1.5 copy-start.33
  549.2 1.5 copy-start.34
  549.3 1.5 copy-start.36
  562.1 418.5 %all-reduce.6.cloned.1.call-start = ((), (), s32[]{:S(2)}) async-start(), calls=%async_computation.4 | async-start | bytes 524288 | tf_op jit(solution)/shard_map/psum | solution.py:75
Sparse Core Ops, SparseCore 0:
  90.4 175.4 all-reduce.3
  269.2 75.8 all-gather.1
  562.2 109.3 reduce-scatter.1
  674.3 306.2 all-reduce.5
where the time goes:
time: 992 us; the launch traced here: 989 us
  waiting for transfers between devices  634 us (64%)
  local copies, waits for them, and re-layouts  94.5 us (10%)
  blocking collectives  82.3 us (8%)
  other arithmetic  56.7 us (6%)
  matrix products  46.3 us (5%)
  loops' own time  40.4 us (4%)
  between operations  34.2 us (3%)
    psum x1, waiting for transfers between devices, local(): return lax.psum(summed, 'row')  309 us
    psum x1, waiting for transfers between devices, from_root(): return lax.psum(kept, axis)  136 us
    reduce_scatter x1, waiting for transfers between devices, local(): summed = lax.psum_scatter(result, 'col', scatter_dimension=0, tiled=True)  109 us
    another operation x16, local copies, waits for them, and re-layouts  86.8 us
    all_gather x1, blocking collectives, local(): col_block = lax.all_gather(pieces, 'row', axis=1, tiled=True)  82.3 us
    all_gather x1, waiting for transfers between devices, local(): shards = lax.all_gather(col_block, 'col', axis=0, tiled=True)  79.2 us
    another operation x16, loops' own time, local(): row_term, col_term = lax.cond(inside, compute, skipped, col_vectors)  40.4 us
    dot_general x16, matrix products, tile_terms(): lax.dot_general(row_vectors, col_vectors, (((1,), (1,)), ((), ())), prefe...  21.7 us
  transfers between devices with their start and end apart: 4, of which 4 were waited for; matrix products, arithmetic and copies ran while one was open for 2% of the time, Pallas kernels for 0%

commit v1 on v0

--- a/solution.py
+++ b/solution.py
@@ -72,7 +72,7 @@
         )
     result = result + jnp.where((block_ids == own_block)[:, None, None], visit_row_sum[None], 0.0)
     summed = lax.psum_scatter(result, "col", scatter_dimension=0, tiled=True)
-    return lax.psum(summed, "row")
+    return jnp.sum(lax.all_gather(summed, "row"), axis=0)
 
 
 def solution(mesh):

time: 992 us -> 879 us (0.89)
  waiting for transfers between devices: 634 us -> 518 us
    psum x1 -> x0, waiting for transfers between devices: 309 us -> none  [local(): return lax.psum(summed, 'row')]
    all_gather x0 -> x1, waiting for transfers between devices: none -> 193 us  [local(): return jnp.sum(lax.all_gather(summed, 'row'), axis=0)]
where the time goes in v1:
time: 879 us; the launch traced here: 876 us
  waiting for transfers between devices  518 us (59%)
  local copies, waits for them, and re-layouts  92.9 us (11%)
  blocking collectives  82.3 us (9%)
  other arithmetic  61.4 us (7%)
  matrix products  46.3 us (5%)
  loops' own time  40.4 us (5%)
  between operations  34.2 us (4%)
    all_gather x1, waiting for transfers between devices, local(): return jnp.sum(lax.all_gather(summed, 'row'), axis=0)  193 us
    psum x1, waiting for transfers between devices, from_root(): return lax.psum(kept, axis)  136 us
    reduce_scatter x1, waiting for transfers between devices, local(): summed = lax.psum_scatter(result, 'col', scatter_dimension=0, tiled=True)  109 us
    another operation x16, local copies, waits for them, and re-layouts  86.8 us
    all_gather x1, blocking collectives, local(): col_block = lax.all_gather(pieces, 'row', axis=1, tiled=True)  82.3 us
    all_gather x1, waiting for transfers between devices, local(): shards = lax.all_gather(col_block, 'col', axis=0, tiled=True)  79.2 us
    another operation x16, loops' own time, local(): row_term, col_term = lax.cond(inside, compute, skipped, col_vectors)  40.4 us
    dot_general x16, matrix products, tile_terms(): lax.dot_general(row_vectors, col_vectors, (((1,), (1,)), ((), ())), prefe...  21.7 us
  transfers between devices with their start and end apart: 4, of which 4 were waited for; matrix products, arithmetic and copies ran while one was open for 2% of the time, Pallas kernels for 0%

profile of v1, /device:TPU:2, one launch (start us, length us, event | category | flops | bytes accessed | tf_op | source)
XLA Modules:
  0.0 875.6 jit_solution(2514432524063847271)
XLA Ops:
  7.2 82.3 %all_gather.12 = bf16[1,256,256]{2,1,0:T(8,128)(2,1)S(1)} all-gather(bf16[1,8,256]{2,1,0:T(8,128)(2,1)S(1)} %convert_element_type.204), channel_id=1, replica_groups=mesh['row'=32,'col'=16] {'row'}, dimensions={1}, use_global_device_ids=true | all-gather | bytes 135168 | tf_op jit(solution)/shard_map/all_gather | solution.py:45
  91.1 2.0 fusion.207
  112.9 1.4 reduce_sum.20
  117.5 1.8 iota_compare_fusion.3
  119.4 1.8 iota_compare_fusion.5
  121.2 1.8 iota_compare_fusion.7
  123.0 1.7 iota_compare_fusion.9
  124.6 1.8 iota_compare_fusion.11
  126.4 1.8 iota_compare_fusion.13
  128.2 1.9 iota_compare_fusion.15
  130.1 135.8 %all-reduce.3.cloned.1.call-done = bf16[256,256]{1,0:T(8,128)(2,1)} async-done(((bf16[256,256]{1,0:T(8,128)(2,1)}), bf16[256,256]{1,0:T(8,128)(2,1)}) %all-reduce.3.cloned.1.call-update) | async-done | bytes 131088 | tf_op jit(solution)/shard_map/psum | solution.py:12
  265.9 79.2 %all-gather.4.cloned.1.call-done = bf16[16,256,256]{2,1,0:T(8,128)(2,1)} async-done(((bf16[1,256,256]{2,1,0:T(8,128)(2,1)}), bf16[16,256,256]{2,1,0:T(8,128)(2,1)}) %all-gather.4.cloned.1.call-update) | async-done | bytes 2097168 | tf_op jit(solution)/shard_map/all_gather | solution.py:48
  345.1 13.3 %conditional.16 = (f32[256,256]{1,0:T(8,128)S(1)}, f32[16,256,256]{2,1,0:T(8,128)}) conditional(s32[]{:T(128)} %convert_element_type.203, () %tuple.261, (s32[1,1,16,256,256]{4,3,2,1,0:T(8,128)}, s32[]{:T(128)}, bf16[16,256,256]{2,1,0:T(8,128)(2,1)}, bf16[256,256]{1,0:T(8,128)(2,1)}, f32[]{:T(128)}, /*index=5*/f32[1,256]{1,0:T(1,128)S(1)}, ...), branch_computations={%region_2.3_spmd, %region_3.4_spmd} | conditional | flops 101646592 | bytes 15079546 | solution.py:64
  347.8 5.4 copy.21
  353.2 1.4 fusion.4
  354.8 2.4 scatter-add.14
  358.4 10.6 %conditional.17 = (f32[256,256]{1,0:T(8,128)S(1)}, f32[1,256,256]{2,1,0:T(8,128)S(1)}) conditional(s32[]{:T(128)} %convert_element_type.207, () %tuple.263, (s32[1,1,16,256,256]{4,3,2,1,0:T(8,128)}, s32[]{:T(128)}, bf16[16,256,256]{2,1,0:T(8,128)(2,1)}, bf16[256,256]{1,0:T(8,128)(2,1)}, f32[]{:T(128)}, /*index=5*/f32[1,256]{1,0:T(1,128)S(1)}, ...), branch_computations={%region_4.5_spmd, %region_5.6_spmd} | conditional | flops 101646592 | bytes 10623094 | solution.py:64
  360.9 5.4 copy.22
  369.8 10.9 %conditional.18 = (f32[256,256]{1,0:T(8,128)S(1)}, f32[1,256,256]{2,1,0:T(8,128)S(1)}) conditional(s32[]{:T(128)} %convert_element_type.208, () %tuple.265, (s32[1,1,16,256,256]{4,3,2,1,0:T(8,128)}, s32[]{:T(128)}, bf16[16,256,256]{2,1,0:T(8,128)(2,1)}, bf16[256,256]{1,0:T(8,128)(2,1)}, f32[]{:T(128)}, /*index=5*/f32[1,256]{1,0:T(1,128)S(1)}, ...), branch_computations={%region_6.7_spmd, %region_7.8_spmd} | conditional | flops 101646592 | bytes 10623094 | solution.py:64
  372.5 5.4 copy.23
  380.7 1.7 fusion.204
  382.4 10.6 %conditional.19 = (f32[256,256]{1,0:T(8,128)S(1)}, f32[1,256,256]{2,1,0:T(8,128)S(1)}) conditional(s32[]{:T(128)} %convert_element_type.209, () %tuple.267, (s32[1,1,16,256,256]{4,3,2,1,0:T(8,128)}, s32[]{:T(128)}, bf16[16,256,256]{2,1,0:T(8,128)(2,1)}, bf16[256,256]{1,0:T(8,128)(2,1)}, f32[]{:T(128)}, /*index=5*/f32[1,256]{1,0:T(1,128)S(1)}, ...), branch_computations={%region_8.9_spmd, %region_9.10_spmd} | conditional | flops 101646592 | bytes 10623094 | solution.py:64
  384.9 5.4 copy.24
  393.0 1.7 fusion.203
  394.7 10.6 %conditional.20 = (f32[256,256]{1,0:T(8,128)S(1)}, f32[1,256,256]{2,1,0:T(8,128)S(1)}) conditional(s32[]{:T(128)} %convert_element_type.210, () %tuple.269, (s32[1,1,16,256,256]{4,3,2,1,0:T(8,128)}, s32[]{:T(128)}, bf16[16,256,256]{2,1,0:T(8,128)(2,1)}, bf16[256,256]{1,0:T(8,128)(2,1)}, f32[]{:T(128)}, /*index=5*/f32[1,256]{1,0:T(1,128)S(1)}, ...), branch_computations={%region_10.11_spmd, %region_11.12_spmd} | conditional | flops 101646592 | bytes 10623094 | solution.py:64
  397.2 5.4 copy.25
  405.3 1.7 fusion.202
  407.0 10.4 %conditional.21 = (f32[256,256]{1,0:T(8,128)S(1)}, f32[1,256,256]{2,1,0:T(8,128)S(1)}) conditional(s32[]{:T(128)} %convert_element_type.211, () %tuple.271, (s32[1,1,16,256,256]{4,3,2,1,0:T(8,128)}, s32[]{:T(128)}, bf16[16,256,256]{2,1,0:T(8,128)(2,1)}, bf16[256,256]{1,0:T(8,128)(2,1)}, f32[]{:T(128)}, /*index=5*/f32[1,256]{1,0:T(1,128)S(1)}, ...), branch_computations={%region_12.13_spmd, %region_13.14_spmd} | conditional | flops 101646592 | bytes 10623094 | solution.py:64
  409.3 5.4 copy.26
  417.4 1.7 fusion.201
  419.1 10.4 %conditional.22 = (f32[256,256]{1,0:T(8,128)S(1)}, f32[1,256,256]{2,1,0:T(8,128)S(1)}) conditional(s32[]{:T(128)} %convert_element_type.212, () %tuple.273, (s32[1,1,16,256,256]{4,3,2,1,0:T(8,128)}, s32[]{:T(128)}, bf16[16,256,256]{2,1,0:T(8,128)(2,1)}, bf16[256,256]{1,0:T(8,128)(2,1)}, f32[]{:T(128)}, /*index=5*/f32[1,256]{1,0:T(1,128)S(1)}, ...), branch_computations={%region_14.15_spmd, %region_15.16_spmd} | conditional | flops 101646592 | bytes 10623094 | solution.py:64
  421.4 5.4 copy.27
  429.5 1.7 fusion.200
  431.2 10.4 %conditional.23 = (f32[256,256]{1,0:T(8,128)S(1)}, f32[1,256,256]{2,1,0:T(8,128)S(1)}) conditional(s32[]{:T(128)} %convert_element_type.213, () %tuple.275, (s32[1,1,16,256,256]{4,3,2,1,0:T(8,128)}, s32[]{:T(128)}, bf16[16,256,256]{2,1,0:T(8,128)(2,1)}, bf16[256,256]{1,0:T(8,128)(2,1)}, f32[]{:T(128)}, /*index=5*/f32[1,256]{1,0:T(1,128)S(1)}, ...), branch_computations={%region_16.17_spmd, %region_17.18_spmd} | conditional | flops 101646592 | bytes 10623094 | solution.py:64
  433.5 5.4 copy.28
  441.6 1.7 fusion.199
  443.3 10.8 %conditional.24 = (f32[256,256]{1,0:T(8,128)S(1)}, f32[1,256,256]{2,1,0:T(8,128)S(1)}) conditional(s32[]{:T(128)} %convert_element_type.214, () %tuple.277, (s32[1,1,16,256,256]{4,3,2,1,0:T(8,128)}, s32[]{:T(128)}, bf16[16,256,256]{2,1,0:T(8,128)(2,1)}, bf16[256,256]{1,0:T(8,128)(2,1)}, f32[]{:T(128)}, /*index=5*/f32[1,256]{1,0:T(1,128)S(1)}, ...), branch_computations={%region_18.19_spmd, %region_19.20_spmd} | conditional | flops 101646592 | bytes 10623094 | solution.py:64
  446.0 5.4 copy.29
  454.1 1.7 fusion.198
  455.8 10.6 %conditional.25 = (f32[256,256]{1,0:T(8,128)S(1)}, f32[1,256,256]{2,1,0:T(8,128)S(1)}) conditional(s32[]{:T(128)} %convert_element_type.215, () %tuple.279, (s32[1,1,16,256,256]{4,3,2,1,0:T(8,128)}, s32[]{:T(128)}, bf16[16,256,256]{2,1,0:T(8,128)(2,1)}, bf16[256,256]{1,0:T(8,128)(2,1)}, f32[]{:T(128)}, /*index=5*/f32[1,256]{1,0:T(1,128)S(1)}, ...), branch_computations={%region_20.21_spmd, %region_21.22_spmd} | conditional | flops 101646592 | bytes 10623094 | solution.py:64
  458.3 5.4 copy.30
  466.4 1.7 fusion.197
  468.2 10.5 %conditional.26 = (f32[256,256]{1,0:T(8,128)S(1)}, f32[1,256,256]{2,1,0:T(8,128)S(1)}) conditional(s32[]{:T(128)} %convert_element_type.216, () %tuple.281, (s32[1,1,16,256,256]{4,3,2,1,0:T(8,128)}, s32[]{:T(128)}, bf16[16,256,256]{2,1,0:T(8,128)(2,1)}, bf16[256,256]{1,0:T(8,128)(2,1)}, f32[]{:T(128)}, /*index=5*/f32[1,256]{1,0:T(1,128)S(1)}, ...), branch_computations={%region_22.23_spmd, %region_23.24_spmd} | conditional | flops 101646592 | bytes 10623094 | solution.py:64
  470.5 5.4 copy.31
  478.6 1.7 fusion.196
  480.3 10.9 %conditional.27 = (f32[256,256]{1,0:T(8,128)S(1)}, f32[1,256,256]{2,1,0:T(8,128)S(1)}) conditional(s32[]{:T(128)} %convert_element_type.217, () %tuple.283, (s32[1,1,16,256,256]{4,3,2,1,0:T(8,128)}, s32[]{:T(128)}, bf16[16,256,256]{2,1,0:T(8,128)(2,1)}, bf16[256,256]{1,0:T(8,128)(2,1)}, f32[]{:T(128)}, /*index=5*/f32[1,256]{1,0:T(1,128)S(1)}, ...), branch_computations={%region_24.25_spmd, %region_25.26_spmd} | conditional | flops 101646592 | bytes 10623094 | solution.py:64
  483.1 5.4 copy.32
  491.3 1.7 fusion.195
  493.0 12.3 %conditional.28 = (f32[256,256]{1,0:T(8,128)S(1)}, f32[1,256,256]{2,1,0:T(8,128)}) conditional(s32[]{:T(128)} %convert_element_type.218, () %tuple.285, (s32[1,1,16,256,256]{4,3,2,1,0:T(8,128)}, s32[]{:T(128)}, bf16[16,256,256]{2,1,0:T(8,128)(2,1)}, bf16[256,256]{1,0:T(8,128)(2,1)}, f32[]{:T(128)}, /*index=5*/f32[1,256]{1,0:T(1,128)S(1)}, ...), branch_computations={%region_26.27_spmd, %region_27.28_spmd} | conditional | flops 101646592 | bytes 10623094 | solution.py:64
  496.4 5.4 copy.33
  505.3 1.9 fusion.205
  507.1 13.3 %conditional.29 = (f32[256,256]{1,0:T(8,128)}, f32[1,256,256]{2,1,0:T(8,128)}) conditional(s32[]{:T(128)} %convert_element_type.219, () %tuple.287, (s32[1,1,16,256,256]{4,3,2,1,0:T(8,128)}, s32[]{:T(128)}, bf16[16,256,256]{2,1,0:T(8,128)(2,1)}, bf16[256,256]{1,0:T(8,128)(2,1)}, f32[]{:T(128)}, /*index=5*/f32[1,256]{1,0:T(1,128)S(1)}, ...), branch_computations={%region_28.29_spmd, %region_29.30_spmd} | conditional | flops 101646592 | bytes 10623094 | solution.py:64
  511.0 5.4 copy.34
  518.6 1.8 fusion.161
  520.5 13.3 %conditional.30 = (f32[256,256]{1,0:T(8,128)}, f32[1,256,256]{2,1,0:T(8,128)}) conditional(s32[]{:T(128)} %convert_element_type.220, () %tuple.289, (s32[1,1,16,256,256]{4,3,2,1,0:T(8,128)}, s32[]{:T(128)}, bf16[16,256,256]{2,1,0:T(8,128)(2,1)}, bf16[256,256]{1,0:T(8,128)(2,1)}, f32[]{:T(128)}, /*index=5*/f32[1,256]{1,0:T(1,128)S(1)}, ...), branch_computations={%region_30.31_spmd, %region_31.32_spmd} | conditional | flops 101646592 | bytes 10623094 | solution.py:64
  524.3 5.4 copy.35
  531.9 1.9 fusion.173
  533.8 11.7 %conditional.31 = (f32[256,256]{1,0:T(8,128)S(1)}, f32[1,256,256]{2,1,0:T(8,128)S(1)}) conditional(s32[]{:T(128)} %convert_element_type.221, () %tuple.291, (s32[1,1,16,256,256]{4,3,2,1,0:T(8,128)}, s32[]{:T(128)}, bf16[16,256,256]{2,1,0:T(8,128)(2,1)}, bf16[256,256]{1,0:T(8,128)(2,1)}, f32[]{:T(128)}, /*index=5*/f32[1,256]{1,0:T(1,128)S(1)}, ...), branch_computations={%region_32.33_spmd, %region_33.34_spmd} | conditional | flops 101646592 | bytes 10627218 | solution.py:64
  537.4 5.4 copy.36
  546.3 2.8 slice_bitcast_fusion.11
  550.7 11.3 %select_add_fusion = f32[16,256,256]{2,1,0:T(8,128)} fusion(f32[256,256]{1,0:T(8,128)S(1)} %add_add_fusion, f32[256,256]{1,0:T(8,128)S(1)} %get-tuple-element.1640, f32[256,256]{1,0:T(8,128)S(1)} %get-tuple-element.1641, f32[256,256]{1,0:T(8,128)S(1)} %get-tuple-element.1642, f32[256,256]{1,0:T(8,128)S(1)} %copy-done.20, ...), kind=kLoop, calls=%fused_computation.288 | loop fusion | flops 34603008 | bytes 8651024 | tf_op jit(solution)/shard_map/add | solution.py:73
  562.1 109.4 %reduce-scatter.2.cloned.1.call-done = f32[1,256,256]{2,1,0:T(8,128)} async-done(((f32[16,256,256]{2,1,0:T(8,128)}), f32[1,256,256]{2,1,0:T(8,128)}) %reduce-scatter.2.cloned.1.call-update) | async-done | bytes 262160 | tf_op jit(solution)/shard_map/reduce_scatter | solution.py:74
  671.6 192.9 %all-gather.6.cloned.1.call-done = f32[32,256,256]{2,1,0:T(8,128)} async-done(((f32[1,256,256]{2,1,0:T(8,128)}), f32[32,256,256]{2,1,0:T(8,128)}) %all-gather.6.cloned.1.call-update) | async-done | bytes 8388624 | tf_op jit(solution)/shard_map/all_gather | solution.py:75
  864.5 4.6 reduce.33
  (152 shorter events, 53.6 us)
Async XLA Ops:
  6.5 259.4 %all-reduce.3.cloned.1.call-start = ((), (), s32[]{:S(2)}) async-start(), calls=%async_computation.2 | async-start | bytes 262144 | tf_op jit(solution)/shard_map/psum | solution.py:12
  89.5 0.8 copy-start.16
  90.3 254.8 %all-gather.4.cloned.1.call-start = ((), (), s32[]{:S(2)}) async-start(), calls=%async_computation.1 | async-start | bytes 2228224 | tf_op jit(solution)/shard_map/all_gather | solution.py:48
  91.0 580.5 %reduce-scatter.2.cloned.1.call-start = ((), (), s32[]{:S(2)}) async-start(), calls=%async_computation.3 | async-start | bytes 4456448 | tf_op jit(solution)/shard_map/reduce_scatter | solution.py:74
  115.1 365.3 %copy-start.21 = (f32[16,256]{1,0:T(8,128)}, f32[16,256]{1,0:T(8,128)S(1)}, u32[]{:S(2)}) copy-start(f32[16,256]{1,0:T(8,128)S(1)} %reshape.990) | copy-start | bytes 49156
  347.8 5.4 copy-start
  360.9 5.4 copy-start.1
  372.5 5.4 copy-start.2
  384.9 5.4 copy-start.3
  397.2 5.4 copy-start.4
  409.3 5.4 copy-start.5
  421.4 5.4 copy-start.6
  433.5 5.4 copy-start.7
  446.0 5.4 copy-start.8
  458.3 5.4 copy-start.9
  470.5 5.4 copy-start.10
  483.1 5.4 copy-start.11
  496.4 5.4 copy-start.12
  511.0 5.4 copy-start.13
  524.2 5.4 copy-start.14
  537.3 5.5 copy-start.15
  537.3 5.5 copy-start.35
  545.5 0.7 copy-start.17
  545.5 0.8 copy-start.19
  546.3 3.0 copy-start.18
  549.1 1.5 copy-start.20
  549.1 1.5 copy-start.22
  549.1 1.5 copy-start.23
  549.1 1.5 copy-start.24
  549.2 1.5 copy-start.25
  549.2 1.5 copy-start.26
  549.2 1.5 copy-start.27
  549.2 1.5 copy-start.28
  549.2 1.5 copy-start.29
  549.2 1.5 copy-start.30
  549.2 1.5 copy-start.31
  549.2 1.5 copy-start.32
  549.2 1.5 copy-start.33
  549.2 1.5 copy-start.34
  549.3 1.5 copy-start.36
  562.1 302.4 %all-gather.6.cloned.1.call-start = ((), (), s32[]{:S(2)}) async-start(), calls=%async_computation.4 | async-start | bytes 8650752 | tf_op jit(solution)/shard_map/all_gather | solution.py:75
Sparse Core Ops, SparseCore 0:
  90.4 175.4 all-reduce.2
  269.2 75.8 all-gather.3
  562.2 109.3 reduce-scatter.1
  673.5 190.9 all-gather.5
